TPU v7x, 32 devices: a whole 2x2x4 slice. The times are simulated.
32 devices in a mesh: tp: 8 (over y, x, core), dp: 4 (over z).
Axes of the slice: x: 2, y: 2, z: 4, core: 2. Of those that a mesh axis runs over, the one named last changes fastest.
Arguments:
- activations: bfloat16 [64, 512, 4096], P('dp', None, 'tp'), may hold values from -6 to 6
- query_output_cotangent: bfloat16 [64, 512, 4096], P('dp', None, 'tp'), may hold values from -6 to 6
- value_output_cotangent: bfloat16 [64, 512, 4096], P('dp', None, 'tp'), may hold values from -6 to 6
- lengths: int32 [64], P('dp'), may hold values from 1 to 512
- reducing_matrices_pair: bfloat16 [2, 4096, 128], P(None, 'tp'), may hold values from -0.09375 to 0.09375
- expanding_matrices_pair: bfloat16 [2, 128, 4096], P(None, None, 'tp'), may hold values from -0.5 to 0.5
- width_side_projections: bfloat16 [2, 4096, 128], P(None, 'tp'), may hold values from -0.09375 to 0.09375
- narrow_random_sketch: bfloat16 [128, 16], replicated, may hold values from -0.5 to 0.5
- projected_first_moment: float32 [8192], replicated, may hold values from -6 to 6
- projected_second_moment: float32 [8192], replicated, may hold values from 0.1 to 10
- targets: bfloat16 [1024, 8192], P('dp', 'tp'), may hold values from -6 to 6
Outputs:
- scores: float32 [64, 1024], P('dp', 'tp')
All inputs are finite; a program needn't handle non-finite values.
Results may differ from a plain program's by a relative error of at most 0.023.
Values may be sent and summed in bfloat16 or wider, within the bound.
A program may use at most 128 MiB of HBM per device.

v0:
```python
import math
import jax
import jax.numpy as jnp
from jax import lax
from jax.sharding import PartitionSpec as P


def adam_update(features, first_moment, second_moment):
    mixed = 0.9 * first_moment + 0.1 * features
    spread = 0.999 * second_moment + 0.001 * features * features
    return mixed / (jnp.sqrt(spread) + 1e-08)


def combine_factors(reducing_matrices_pair, expanding_matrices_pair, narrow_random_sketch):
    attention_key_reducer = jnp.dot(
        reducing_matrices_pair[0], narrow_random_sketch, preferred_element_type=jnp.float32
    ).astype(jnp.bfloat16)
    value_down_factor = jnp.dot(
        reducing_matrices_pair[1], narrow_random_sketch, preferred_element_type=jnp.float32
    ).astype(jnp.bfloat16)
    query_up_factor = jnp.dot(
        expanding_matrices_pair[0].T, narrow_random_sketch, preferred_element_type=jnp.float32
    ).astype(jnp.bfloat16)
    value_up_factor = jnp.dot(
        expanding_matrices_pair[1].T, narrow_random_sketch, preferred_element_type=jnp.float32
    ).astype(jnp.bfloat16)
    return (attention_key_reducer, value_down_factor, query_up_factor, value_up_factor)


def body(
    activations,
    query_output_cotangent,
    value_output_cotangent,
    lengths,
    reducing_matrices_pair,
    expanding_matrices_pair,
    width_side_projections,
    narrow_random_sketch,
    projected_first_moment,
    projected_second_moment,
    targets,
):
    attention_key_reducer, value_down_factor, query_up_factor, value_up_factor = combine_factors(
        reducing_matrices_pair, expanding_matrices_pair, narrow_random_sketch
    )
    rank_cols = narrow_random_sketch.shape[1]
    w_left = jnp.concatenate(
        [attention_key_reducer, value_down_factor, width_side_projections[0]], axis=1
    )
    w_query = jnp.concatenate([query_up_factor, width_side_projections[1]], axis=1)
    w_value = jnp.concatenate([value_up_factor, width_side_projections[1]], axis=1)
    groups = lax.axis_size("tp")
    parts = lax.axis_size("dp")
    member = lax.axis_index("tp")
    local_ex, seq_len = activations.shape[:2]
    feature_count = projected_first_moment.shape[0]
    positions = jnp.arange(seq_len, dtype=jnp.int32)
    token_mask = (positions[None, :] < lengths[:, None])[..., None]

    def project(rows, weights):
        out = jnp.einsum("esd,dc->esc", rows, weights, preferred_element_type=jnp.float32)
        return out.astype(jnp.bfloat16)

    left = project(activations, w_left)
    right_q = project(query_output_cotangent, w_query)
    right_v = project(value_output_cotangent, w_value)
    narrow = jnp.concatenate(
        [left[..., : 2 * rank_cols], right_q[..., :rank_cols], right_v[..., :rank_cols]], axis=-1
    )
    narrow = jnp.where(token_mask, narrow, jnp.zeros((), jnp.bfloat16))
    narrow = lax.psum(narrow, "tp")

    def outer_sum(first, wide):
        return jnp.einsum(
            "esr,esk->erk",
            narrow[..., first * rank_cols : (first + 1) * rank_cols],
            wide,
            preferred_element_type=jnp.float32,
        )

    own_features = jnp.concatenate(
        [
            outer_sum(2, left[..., 2 * rank_cols :]),
            outer_sum(3, left[..., 2 * rank_cols :]),
            outer_sum(0, right_q[..., rank_cols:]),
            outer_sum(1, right_v[..., rank_cols:]),
        ],
        axis=1,
    ).reshape(local_ex, -1)
    features = lax.psum_scatter(
        own_features.astype(jnp.bfloat16), "tp", scatter_dimension=1, tiled=True
    ).astype(jnp.float32)
    span = feature_count // groups
    first_moment = lax.dynamic_slice_in_dim(projected_first_moment, member * span, span)
    second_moment = lax.dynamic_slice_in_dim(projected_second_moment, member * span, span)
    update = adam_update(features, first_moment, second_moment).astype(jnp.bfloat16)
    update = lax.all_gather(update, "dp", axis=0, tiled=True)
    wide_update = update.astype(jnp.float32)
    target_float = targets.astype(jnp.float32)
    update_sq = jnp.sum(wide_update * wide_update, axis=1)
    target_sq = jnp.sum(target_float * target_float, axis=1)
    dots = lax.dot_general(
        update, targets, (((1,), (1,)), ((), ())), preferred_element_type=jnp.float32
    )
    rows = jnp.concatenate(
        [dots, jnp.broadcast_to(update_sq[:, None], (dots.shape[0], 128))], axis=1
    ).reshape(parts, local_ex, -1)
    extra = jnp.pad(target_sq, (0, 128))
    rows = jnp.concatenate([rows, jnp.broadcast_to(extra, (parts, 8, extra.shape[0]))], axis=1)
    rows = lax.psum(rows, "tp")
    rows = lax.all_to_all(rows, "dp", split_axis=0, concat_axis=0, tiled=True)
    owned = targets.shape[0]
    totals = jnp.moveaxis(rows[:, :, :owned], 0, 1).reshape(local_ex + 8, parts * owned)
    columns = parts * owned // groups
    totals = lax.dynamic_slice_in_dim(totals, member * columns, columns, 1)
    row_scale = lax.rsqrt(rows[0, :local_ex, owned : owned + 1] + 1e-06)
    column_scale = lax.rsqrt(totals[local_ex : local_ex + 1] + 1e-06)
    return totals[:local_ex] * row_scale * column_scale * math.sqrt(feature_count)


def solution(mesh):
    placed = (
        P("dp", None, "tp"),
        P("dp", None, "tp"),
        P("dp", None, "tp"),
        P("dp"),
        P(None, "tp", None),
        P(None, None, "tp"),
        P(None, "tp", None),
        P(),
        P(),
        P(),
        P("dp", "tp"),
    )
    return jax.shard_map(body, mesh=mesh, in_specs=placed, out_specs=P("dp", "tp"), check_vma=False)
```

profile of v0, /device:TPU:0, one launch (start us, length us, event | category | flops | bytes accessed | tf_op | source)
XLA Modules:
  0.0 220.2 jit_solution(16352123582546980845)
XLA Ops:
  6.5 0.0 copy-start
  6.5 0.7 copy-done
  7.2 1.0 convolution_convert_fusion.2
  8.3 1.1 convolution_convert_fusion.3
  9.3 1.0 convolution_convert_fusion.1
  10.4 1.0 convolution_convert_fusion
  11.4 1.0 fusion.55
  12.4 0.1 copy.37
  12.5 6.3 %convert_bitcast_fusion = bf16[16,512,160]{1,2,0:T(8,128)(2,1)S(1)} fusion(bf16[16,512,512]{2,1,0:T(8,128)(2,1)} %param.11, bf16[512,128]{0,1:T(8,128)(2,1)S(1)} %bitcast.53, bf16[512,16]{0,1:T(8,128)(2,1)S(1)} %convolution_convert_fusion.2, bf16[512,16]{0,1:T(8,128)(2,1)S(1)} %convolution_convert_fusion.3), kind=kOutput, calls=%fused_computation | convolution fusion | flops 1343979520 | bytes 11173888 | tf_op jit(solution)/shard_map/esd,dc->esc/dot_general | solution.py:61
  18.8 0.0 copy-start.1
  18.8 0.1 copy.38
  18.9 7.1 %convert_bitcast_fusion.2 = bf16[16,512,144]{1,2,0:T(8,128)(2,1)S(1)} fusion(bf16[16,512,512]{2,1,0:T(8,128)(2,1)} %param.12, bf16[512,16]{0,1:T(8,128)(2,1)S(1)} %convolution_convert_fusion.1, bf16[512,128]{0,1:T(8,128)(2,1)S(1)} %bitcast.49), kind=kOutput, calls=%fused_computation.2 | convolution fusion | flops 1209434112 | bytes 10895360 | tf_op jit(solution)/shard_map/esd,dc->esc/dot_general | solution.py:61
  26.1 0.0 copy-start.8
  26.1 0.0 slice-start
  26.1 7.1 %convert_bitcast_fusion.1 = bf16[16,512,144]{1,2,0:T(8,128)(2,1)S(1)} fusion(bf16[16,512,512]{2,1,0:T(8,128)(2,1)} %param.13, bf16[512,16]{0,1:T(8,128)(2,1)S(1)} %convolution_convert_fusion, bf16[512,128]{0,1:T(8,128)(2,1)S(1)} %bitcast.50), kind=kOutput, calls=%fused_computation.1 | convolution fusion | flops 1209434112 | bytes 10895360 | tf_op jit(solution)/shard_map/esd,dc->esc/dot_general | solution.py:61
  33.2 0.0 copy-done.3
  33.2 0.0 copy-start.5
  33.2 0.0 copy-start.2
  33.2 1.4 copy-done.5
  34.6 0.1 iota_compare_fusion
  34.7 1.3 maximum_select_fusion
  36.0 0.0 all-reduce.4.cloned.1.call-update
  36.0 0.0 reduce-scatter.2.cloned.1.call-start
  36.1 59.4 %all-reduce.4.cloned.1.call-done = bf16[16,512,64]{1,2,0:T(8,128)(2,1)} async-done(((bf16[16,512,64]{1,2,0:T(8,128)(2,1)}), bf16[16,512,64]{1,2,0:T(8,128)(2,1)}) %all-reduce.4.cloned.1.call-update) | async-done | bytes 1048592 | tf_op jit(solution)/shard_map/psum | solution.py:71
  95.5 1.7 fusion.8
  97.2 1.8 fusion.11
  99.0 0.0 copy-done.9
  99.0 0.0 copy-start.7
  99.0 0.6 fusion.14
  99.7 0.7 fusion.17
  100.4 0.9 copy.42
  101.2 0.0 reduce-scatter.2.cloned.1.call-update
  101.3 0.0 all-reduce.6.cloned.1.call-start
  101.3 0.2 multiply_reduce_fusion
  101.5 0.7 dynamic-slice_multiply_fusion.1
  102.2 31.9 %reduce-scatter.2.cloned.1.call-done = bf16[16,1024]{1,0:T(8,128)(2,1)} async-done(((bf16[16,8192]{1,0:T(8,128)(2,1)}), bf16[16,1024]{1,0:T(8,128)(2,1)}) %reduce-scatter.2.cloned.1.call-update) | async-done | bytes 32784 | tf_op jit(solution)/shard_map/reduce_scatter | solution.py:90
  134.1 0.8 fusion.42
  134.9 13.5 %all_gather.3 = bf16[64,1024]{1,0:T(8,128)(2,1)S(1)} all-gather(bf16[16,1024]{1,0:T(8,128)(2,1)S(1)} %fusion.42), channel_id=1, replica_groups=mesh['tp'=8,'dp'=4] {'dp'}, dimensions={0}, use_global_device_ids=true | all-gather | bytes 163840 | tf_op jit(solution)/shard_map/all_gather | solution.py:97
  148.4 0.3 fusion.56
  148.7 0.1 multiply_reduce_fusion.1
  148.8 0.1 broadcast_in_dim.28
  148.9 0.7 pad_maximum_fusion.1
  149.6 0.0 all-reduce.6.cloned.1.call-update
  149.6 52.0 %all-reduce.6.cloned.1.call-done = f32[4,24,384]{2,1,0:T(8,128)} async-done(((f32[4,24,384]{2,1,0:T(8,128)}), f32[4,24,384]{2,1,0:T(8,128)}) %all-reduce.6.cloned.1.call-update) | async-done | bytes 147472 | tf_op jit(solution)/shard_map/psum | solution.py:110
  201.6 4.6 %all-to-all-start = ((f32[4,24,384]{2,1,0:T(8,128)}), f32[4,24,384]{2,1,0:T(8,128)S(1)}, u32[]{:S(2)}, u32[]{:S(2)}) async-start(f32[4,24,384]{2,1,0:T(8,128)} %all-reduce.6.cloned.1.call-done), calls=%async_computation.1 | async-start | bytes 294912 | tf_op jit(solution)/shard_map/all_to_all | solution.py:111
  206.2 6.6 %all-to-all-done = f32[4,24,384]{2,1,0:T(8,128)S(1)} async-done(((f32[4,24,384]{2,1,0:T(8,128)}), f32[4,24,384]{2,1,0:T(8,128)S(1)}, u32[]{:S(2)}, u32[]{:S(2)}) %all-to-all-start) | async-done | bytes 147488 | tf_op jit(solution)/shard_map/all_to_all | solution.py:111
  212.9 0.1 fusion.47
  213.0 0.7 fusion.49
  (21 shorter events, 0.2 us)
Async XLA Ops:
  6.5 0.7 copy-start
  6.5 88.9 %all-reduce.4.cloned.1.call-start = ((), (), s32[]{:S(2)}) async-start(), calls=%async_computation.2 | async-start | bytes 2097152 | tf_op jit(solution)/shard_map/psum | solution.py:71
  18.8 7.2 %copy-start.1 = (bf16[16,512,160]{1,2,0:T(8,128)(2,1)}, bf16[16,512,160]{1,2,0:T(8,128)(2,1)S(1)}, u32[]{:S(2)}) copy-start(bf16[16,512,160]{1,2,0:T(8,128)(2,1)S(1)} %convert_bitcast_fusion) | copy-start | bytes 7864324
  26.0 7.2 %copy-start.3 = (bf16[16,512,144]{1,2,0:T(8,128)(2,1)}, bf16[16,512,144]{1,2,0:T(8,128)(2,1)S(1)}, u32[]{:S(2)}) copy-start(bf16[16,512,144]{1,2,0:T(8,128)(2,1)S(1)} %convert_bitcast_fusion.2) | copy-start | bytes 7077892
  26.1 8.6 %copy-start.8 = (s32[16]{0:T(128)S(1)}, s32[16]{0:T(128)}, u32[]{:S(2)}) copy-start(s32[16]{0:T(128)} %param.14) | copy-start | bytes 196
  26.1 8.6 %slice-start = ((bf16[16,512,160]{1,2,0:T(8,128)(2,1)}), bf16[16,512,32]{1,2,0:T(8,128)(2,1)S(1)}, s32[]{:S(2)}) async-start(bf16[16,512,160]{1,2,0:T(8,128)(2,1)} %copy-done.1), calls=%async_computation.5 | async-start | bytes 1048576 | tf_op jit(solution)/shard_map/slice | solution.py:68
  33.2 1.4 copy-start.5
  33.2 62.3 %copy-start.2 = (bf16[16,512,160]{1,2,0:T(8,128)(2,1)S(1)}, bf16[16,512,160]{1,2,0:T(8,128)(2,1)}, u32[]{:S(2)}) copy-start(bf16[16,512,160]{1,2,0:T(8,128)(2,1)} %copy-done.1) | copy-start | bytes 7864324
  36.0 98.1 %reduce-scatter.2.cloned.1.call-start = ((), (), s32[]{:S(2)}) async-start(), calls=%async_computation.3 | async-start | bytes 294912 | tf_op jit(solution)/shard_map/reduce_scatter | solution.py:90
  95.5 3.5 %copy-start.4 = (bf16[16,512,144]{1,2,0:T(8,128)(2,1)S(1)}, bf16[16,512,144]{1,2,0:T(8,128)(2,1)}, u32[]{:S(2)}) copy-start(bf16[16,512,144]{1,2,0:T(8,128)(2,1)} %copy-done.3) | copy-start | bytes 7077892
  95.5 3.5 %copy-start.9 = (bf16[16,512,64]{1,2,0:T(8,128)(2,1)S(1)}, bf16[16,512,64]{1,2,0:T(8,128)(2,1)}, u32[]{:S(2)}) copy-start(bf16[16,512,64]{1,2,0:T(8,128)(2,1)} %all-reduce.4.cloned.1.call-done) | copy-start | bytes 3145732
  97.2 2.4 %copy-start.6 = (bf16[16,512,144]{1,2,0:T(8,128)(2,1)S(1)}, bf16[16,512,144]{1,2,0:T(8,128)(2,1)}, u32[]{:S(2)}) copy-start(bf16[16,512,144]{1,2,0:T(8,128)(2,1)} %copy-done.5) | copy-start | bytes 7077892
  99.0 2.3 %copy-start.7 = (bf16[256,1024]{1,0:T(8,128)(2,1)S(1)}, bf16[256,1024]{1,0:T(8,128)(2,1)}, u32[]{:S(2)}) copy-start(bf16[256,1024]{1,0:T(8,128)(2,1)} %param.21) | copy-start | bytes 1572868
  101.3 100.4 %all-reduce.6.cloned.1.call-start = ((), (), s32[]{:S(2)}) async-start(), calls=%async_computation.4 | async-start | bytes 294912 | tf_op jit(solution)/shard_map/psum | solution.py:110
  201.6 11.2 %all-to-all-start = ((f32[4,24,384]{2,1,0:T(8,128)}), f32[4,24,384]{2,1,0:T(8,128)S(1)}, u32[]{:S(2)}, u32[]{:S(2)}) async-start(f32[4,24,384]{2,1,0:T(8,128)} %all-reduce.6.cloned.1.call-done), calls=%async_computation.1 | async-start | bytes 294912 | tf_op jit(solution)/shard_map/all_to_all | solution.py:111
Sparse Core Ops, SparseCore 0:
  36.1 59.2 all-reduce.3
  101.4 32.6 reduce-scatter.1
  149.8 51.8 all-reduce.5
where the time goes:
time: 221 us; the launch traced here: 220 us
  waiting for transfers between devices  150 us (68%)
  matrix products  29.7 us (13%)
  blocking collectives  13.5 us (6%)
  between operations  13.3 us (6%)
  other arithmetic  4.71 us (2%)
  starting transfers between devices  4.69 us (2%)
  local copies, waits for them, and re-layouts  4.36 us (2%)
    psum x1, waiting for transfers between devices, body(): narrow = lax.psum(narrow, 'tp')  59.4 us
    psum x1, waiting for transfers between devices, body(): rows = lax.psum(rows, 'tp')  52 us
    reduce_scatter x1, waiting for transfers between devices, body(): lax.psum_scatter(own_features.astype(jnp.bfloat16), 'tp', scatter_dimensi...  31.9 us
    dot_general x3, matrix products, project(): jnp.einsum('esd,dc->esc', rows, weights, preferred_element_type=jnp.float32)  20.4 us
    all_gather x1, blocking collectives, body(): update = lax.all_gather(update, 'dp', axis=0, tiled=True)  13.5 us
    all_to_all x1, waiting for transfers between devices, body(): rows = lax.all_to_all(rows, 'dp', split_axis=0, concat_axis=0, tiled=True)  6.65 us
    dot_general x4, matrix products, outer_sum(): jnp.einsum('esr,esk->erk', narrow[..., first * rank_cols:(first + 1) * ra...  4.82 us
    all_to_all x1, starting transfers between devices, body(): rows = lax.all_to_all(rows, 'dp', split_axis=0, concat_axis=0, tiled=True)  4.6 us
  transfers between devices with their start and end apart: 4, of which 4 were waited for; matrix products, arithmetic and copies ran while one was open for 0% of the time, Pallas kernels for 0%

commit v1 on v0

--- a/solution.py
+++ b/solution.py
@@ -94,7 +94,13 @@
     first_moment = lax.dynamic_slice_in_dim(projected_first_moment, member * span, span)
     second_moment = lax.dynamic_slice_in_dim(projected_second_moment, member * span, span)
     update = adam_update(features, first_moment, second_moment).astype(jnp.bfloat16)
-    update = lax.all_gather(update, "dp", axis=0, tiled=True)
+    peers = lax.axis_size("dp")
+    block, blocks = (update, [update])
+    for _ in range(peers - 1):
+        block = lax.ppermute(block, "dp", [(i, (i + 1) % peers) for i in range(peers)])
+        blocks.insert(0, block)
+    line = jnp.concatenate(blocks, axis=0)
+    update = jnp.roll(line, (lax.axis_index("dp") + 1) * update.shape[0], axis=0)
     wide_update = update.astype(jnp.float32)
     target_float = targets.astype(jnp.float32)
     update_sq = jnp.sum(wide_update * wide_update, axis=1)

time: 221 us -> 224 us (1.014)
  blocking collectives: 13.5 us -> 0 us
  waiting for transfers between devices: 150 us -> 163 us
    ppermute x0 -> x3, waiting for transfers between devices: none -> 15.4 us  [body(): lax.ppermute(block, 'dp', [(i, (i + 1) % peers) for i in range(peers)])]
    all_gather x1 -> x0, blocking collectives: 13.5 us -> none  [body(): update = lax.all_gather(update, 'dp', axis=0, tiled=True)]
    psum x1, waiting for transfers between devices: 52 us -> 49.3 us  [body(): rows = lax.psum(rows, 'tp')]
  transfers between devices with their start and end apart: 4 -> 7, of which waited for: 4 -> 7; matrix products, arithmetic and copies ran while one was open for 0% -> 0% of each run, Pallas kernels for 0% -> 0%
where the time goes in v1:
time: 224 us; the launch traced here: 223 us
  waiting for transfers between devices  163 us (73%)
  matrix products  29.7 us (13%)
  between operations  13.4 us (6%)
  other arithmetic  6.34 us (3%)
  starting transfers between devices  6.22 us (3%)
  local copies, waits for them, and re-layouts  4.39 us (2%)
    psum x1, waiting for transfers between devices, body(): narrow = lax.psum(narrow, 'tp')  59.4 us
    psum x1, waiting for transfers between devices, body(): rows = lax.psum(rows, 'tp')  49.3 us
    reduce_scatter x1, waiting for transfers between devices, body(): lax.psum_scatter(own_features.astype(jnp.bfloat16), 'tp', scatter_dimensi...  32.1 us
    dot_general x3, matrix products, project(): jnp.einsum('esd,dc->esc', rows, weights, preferred_element_type=jnp.float32)  20.4 us
    ppermute x3, waiting for transfers between devices, body(): lax.ppermute(block, 'dp', [(i, (i + 1) % peers) for i in range(peers)])  15.4 us
    all_to_all x1, waiting for transfers between devices, body(): rows = lax.all_to_all(rows, 'dp', split_axis=0, concat_axis=0, tiled=True)  6.65 us
    dot_general x4, matrix products, outer_sum(): jnp.einsum('esr,esk->erk', narrow[..., first * rank_cols:(first + 1) * ra...  4.82 us
    all_to_all x1, starting transfers between devices, body(): rows = lax.all_to_all(rows, 'dp', split_axis=0, concat_axis=0, tiled=True)  4.6 us
  transfers between devices with their start and end apart: 7, of which 7 were waited for; matrix products, arithmetic and copies ran while one was open for 0% of the time, Pallas kernels for 0%

profile of v1, /device:TPU:0, one launch (start us, length us, event | category | flops | bytes accessed | tf_op | source)
XLA Modules:
  0.0 222.9 jit_solution(7167127876675321850)
XLA Ops:
  6.5 0.7 copy-done
  7.2 1.0 convolution_convert_fusion.2
  8.3 1.1 convolution_convert_fusion.3
  9.3 1.0 convolution_convert_fusion.1
  10.4 1.0 convolution_convert_fusion
  11.4 1.0 fusion.58
  12.4 0.1 copy.37
  12.5 6.3 %convert_bitcast_fusion = bf16[16,512,160]{1,2,0:T(8,128)(2,1)S(1)} fusion(bf16[16,512,512]{2,1,0:T(8,128)(2,1)} %param.11, bf16[512,128]{0,1:T(8,128)(2,1)S(1)} %bitcast.52, bf16[512,16]{0,1:T(8,128)(2,1)S(1)} %convolution_convert_fusion.2, bf16[512,16]{0,1:T(8,128)(2,1)S(1)} %convolution_convert_fusion.3), kind=kOutput, calls=%fused_computation | convolution fusion | flops 1343979520 | bytes 11173888 | tf_op jit(solution)/shard_map/esd,dc->esc/dot_general | solution.py:61
  18.8 0.1 copy.38
  18.9 7.1 %convert_bitcast_fusion.2 = bf16[16,512,144]{1,2,0:T(8,128)(2,1)S(1)} fusion(bf16[16,512,512]{2,1,0:T(8,128)(2,1)} %param.12, bf16[512,16]{0,1:T(8,128)(2,1)S(1)} %convolution_convert_fusion.1, bf16[512,128]{0,1:T(8,128)(2,1)S(1)} %bitcast.48), kind=kOutput, calls=%fused_computation.2 | convolution fusion | flops 1209434112 | bytes 10895360 | tf_op jit(solution)/shard_map/esd,dc->esc/dot_general | solution.py:61
  26.1 0.0 copy-start.8
  26.1 0.0 slice-start
  26.1 7.1 %convert_bitcast_fusion.1 = bf16[16,512,144]{1,2,0:T(8,128)(2,1)S(1)} fusion(bf16[16,512,512]{2,1,0:T(8,128)(2,1)} %param.13, bf16[512,16]{0,1:T(8,128)(2,1)S(1)} %convolution_convert_fusion, bf16[512,128]{0,1:T(8,128)(2,1)S(1)} %bitcast.49), kind=kOutput, calls=%fused_computation.1 | convolution fusion | flops 1209434112 | bytes 10895360 | tf_op jit(solution)/shard_map/esd,dc->esc/dot_general | solution.py:61
  33.2 1.4 copy-done.5
  34.6 0.1 iota_compare_fusion
  34.7 1.3 maximum_select_fusion
  36.0 0.0 all-reduce.4.cloned.1.call-update
  36.0 0.0 reduce-scatter.2.cloned.1.call-start
  36.1 59.4 %all-reduce.4.cloned.1.call-done = bf16[16,512,64]{1,2,0:T(8,128)(2,1)} async-done(((bf16[16,512,64]{1,2,0:T(8,128)(2,1)}), bf16[16,512,64]{1,2,0:T(8,128)(2,1)}) %all-reduce.4.cloned.1.call-update) | async-done | bytes 1048592 | tf_op jit(solution)/shard_map/psum | solution.py:71
  95.5 1.7 fusion.8
  97.2 1.8 fusion.11
  99.0 0.0 copy-start.7
  99.0 0.6 fusion.14
  99.7 0.7 fusion.17
  100.4 0.9 copy.42
  101.3 0.0 reduce-scatter.2.cloned.1.call-update
  101.3 0.0 all-reduce.6.cloned.1.call-start
  101.4 0.7 dynamic-slice_multiply_fusion.1
  102.1 32.1 %reduce-scatter.2.cloned.1.call-done = bf16[16,1024]{1,0:T(8,128)(2,1)} async-done(((bf16[16,8192]{1,0:T(8,128)(2,1)}), bf16[16,1024]{1,0:T(8,128)(2,1)}) %reduce-scatter.2.cloned.1.call-update) | async-done | bytes 32784 | tf_op jit(solution)/shard_map/reduce_scatter | solution.py:90
  134.2 0.8 fusion.44
  135.0 1.5 collective-permute-start
  136.5 4.2 %collective-permute-done = bf16[16,1024]{1,0:T(8,128)(2,1)S(1)} collective-permute-done((bf16[16,1024]{1,0:T(8,128)(2,1)S(1)}, bf16[16,1024]{1,0:T(8,128)(2,1)S(1)}, u32[]{:S(2)}, u32[]{:S(2)}) %collective-permute-start) | collective-permute-done | bytes 32800 | tf_op jit(solution)/shard_map/ppermute | solution.py:100
  140.7 0.0 collective-permute-start.1
  140.7 5.7 %collective-permute-done.1 = bf16[16,1024]{1,0:T(8,128)(2,1)S(1)} collective-permute-done((bf16[16,1024]{1,0:T(8,128)(2,1)S(1)}, bf16[16,1024]{1,0:T(8,128)(2,1)S(1)}, u32[]{:S(2)}, u32[]{:S(2)}) %collective-permute-start.1) | collective-permute-done | bytes 32800 | tf_op jit(solution)/shard_map/ppermute | solution.py:100
  146.5 0.2 multiply_reduce_fusion
  146.7 5.5 %collective-permute-done.2 = bf16[16,1024]{1,0:T(8,128)(2,1)S(1)} collective-permute-done((bf16[16,1024]{1,0:T(8,128)(2,1)S(1)}, bf16[16,1024]{1,0:T(8,128)(2,1)S(1)}, u32[]{:S(2)}, u32[]{:S(2)}) %collective-permute-start.2) | collective-permute-done | bytes 32800 | tf_op jit(solution)/shard_map/ppermute | solution.py:100
  152.2 0.8 constant_dynamic-update-slice_fusion.4
  153.0 0.8 constant_dynamic-update-slice_fusion
  153.8 0.3 fusion.40
  154.1 0.1 multiply_reduce_fusion.1
  154.2 0.1 broadcast_in_dim.28
  154.4 0.7 pad_maximum_fusion.1
  155.0 0.0 all-reduce.6.cloned.1.call-update
  155.0 49.3 %all-reduce.6.cloned.1.call-done = f32[4,24,384]{2,1,0:T(8,128)} async-done(((f32[4,24,384]{2,1,0:T(8,128)}), f32[4,24,384]{2,1,0:T(8,128)}) %all-reduce.6.cloned.1.call-update) | async-done | bytes 147472 | tf_op jit(solution)/shard_map/psum | solution.py:116
  204.3 4.6 %all-to-all-start = ((f32[4,24,384]{2,1,0:T(8,128)}), f32[4,24,384]{2,1,0:T(8,128)S(1)}, u32[]{:S(2)}, u32[]{:S(2)}) async-start(f32[4,24,384]{2,1,0:T(8,128)} %all-reduce.6.cloned.1.call-done), calls=%async_computation.1 | async-start | bytes 294912 | tf_op jit(solution)/shard_map/all_to_all | solution.py:117
  208.9 6.6 %all-to-all-done = f32[4,24,384]{2,1,0:T(8,128)S(1)} async-done(((f32[4,24,384]{2,1,0:T(8,128)}), f32[4,24,384]{2,1,0:T(8,128)S(1)}, u32[]{:S(2)}, u32[]{:S(2)}) %all-to-all-start) | async-done | bytes 147488 | tf_op jit(solution)/shard_map/all_to_all | solution.py:117
  215.6 0.1 fusion.49
  215.7 0.7 fusion.51
  (34 shorter events, 0.2 us)
Async XLA Ops:
  6.5 0.7 copy-start
  6.5 89.0 %all-reduce.4.cloned.1.call-start = ((), (), s32[]{:S(2)}) async-start(), calls=%async_computation.2 | async-start | bytes 2097152 | tf_op jit(solution)/shard_map/psum | solution.py:71
  18.8 7.2 %copy-start.1 = (bf16[16,512,160]{1,2,0:T(8,128)(2,1)}, bf16[16,512,160]{1,2,0:T(8,128)(2,1)S(1)}, u32[]{:S(2)}) copy-start(bf16[16,512,160]{1,2,0:T(8,128)(2,1)S(1)} %convert_bitcast_fusion) | copy-start | bytes 7864324
  26.0 7.2 %copy-start.3 = (bf16[16,512,144]{1,2,0:T(8,128)(2,1)}, bf16[16,512,144]{1,2,0:T(8,128)(2,1)S(1)}, u32[]{:S(2)}) copy-start(bf16[16,512,144]{1,2,0:T(8,128)(2,1)S(1)} %convert_bitcast_fusion.2) | copy-start | bytes 7077892
  26.1 8.6 %copy-start.8 = (s32[16]{0:T(128)S(1)}, s32[16]{0:T(128)}, u32[]{:S(2)}) copy-start(s32[16]{0:T(128)} %param.14) | copy-start | bytes 196
  26.1 8.6 %slice-start = ((bf16[16,512,160]{1,2,0:T(8,128)(2,1)}), bf16[16,512,32]{1,2,0:T(8,128)(2,1)S(1)}, s32[]{:S(2)}) async-start(bf16[16,512,160]{1,2,0:T(8,128)(2,1)} %copy-done.1), calls=%async_computation.5 | async-start | bytes 1048576 | tf_op jit(solution)/shard_map/slice | solution.py:68
  33.2 1.4 copy-start.5
  33.2 62.3 %copy-start.2 = (bf16[16,512,160]{1,2,0:T(8,128)(2,1)S(1)}, bf16[16,512,160]{1,2,0:T(8,128)(2,1)}, u32[]{:S(2)}) copy-start(bf16[16,512,160]{1,2,0:T(8,128)(2,1)} %copy-done.1) | copy-start | bytes 7864324
  36.0 98.1 %reduce-scatter.2.cloned.1.call-start = ((), (), s32[]{:S(2)}) async-start(), calls=%async_computation.3 | async-start | bytes 294912 | tf_op jit(solution)/shard_map/reduce_scatter | solution.py:90
  95.5 3.5 %copy-start.4 = (bf16[16,512,144]{1,2,0:T(8,128)(2,1)S(1)}, bf16[16,512,144]{1,2,0:T(8,128)(2,1)}, u32[]{:S(2)}) copy-start(bf16[16,512,144]{1,2,0:T(8,128)(2,1)} %copy-done.3) | copy-start | bytes 7077892
  95.5 3.5 %copy-start.9 = (bf16[16,512,64]{1,2,0:T(8,128)(2,1)S(1)}, bf16[16,512,64]{1,2,0:T(8,128)(2,1)}, u32[]{:S(2)}) copy-start(bf16[16,512,64]{1,2,0:T(8,128)(2,1)} %all-reduce.4.cloned.1.call-done) | copy-start | bytes 3145732
  97.2 2.4 %copy-start.6 = (bf16[16,512,144]{1,2,0:T(8,128)(2,1)S(1)}, bf16[16,512,144]{1,2,0:T(8,128)(2,1)}, u32[]{:S(2)}) copy-start(bf16[16,512,144]{1,2,0:T(8,128)(2,1)} %copy-done.5) | copy-start | bytes 7077892
  99.0 47.4 %copy-start.7 = (bf16[256,1024]{1,0:T(8,128)(2,1)S(1)}, bf16[256,1024]{1,0:T(8,128)(2,1)}, u32[]{:S(2)}) copy-start(bf16[256,1024]{1,0:T(8,128)(2,1)} %param.21) | copy-start | bytes 1572868
  101.3 103.0 %all-reduce.6.cloned.1.call-start = ((), (), s32[]{:S(2)}) async-start(), calls=%async_computation.4 | async-start | bytes 294912 | tf_op jit(solution)/shard_map/psum | solution.py:116
  135.0 5.8 %collective-permute-start = (bf16[16,1024]{1,0:T(8,128)(2,1)S(1)}, bf16[16,1024]{1,0:T(8,128)(2,1)S(1)}, u32[]{:S(2)}, u32[]{:S(2)}) collective-permute-start(bf16[16,1024]{1,0:T(8,128)(2,1)S(1)} %fusion.44), channel_id=1, source_target_pairs={{0,1},{1,2},{2,3},{3,0},{4,5},{5,6},{6,7},{7,4},{8,9},{9,10},{10,1... | collective-permute-start | bytes 98312 | tf_op jit(solution)/shard_map/ppermute | solution.py:100
  140.7 5.7 %collective-permute-start.1 = (bf16[16,1024]{1,0:T(8,128)(2,1)S(1)}, bf16[16,1024]{1,0:T(8,128)(2,1)S(1)}, u32[]{:S(2)}, u32[]{:S(2)}) collective-permute-start(bf16[16,1024]{1,0:T(8,128)(2,1)S(1)} %collective-permute-done), channel_id=1, source_target_pairs={{0,1},{1,2},{2,3},{3,0},{4,5},{5,6},{6,7},{7,4},{8,9},{9,10},{10,1... | collective-permute-start | bytes 98312 | tf_op jit(solution)/shard_map/ppermute | solution.py:100
  146.4 5.7 %collective-permute-start.2 = (bf16[16,1024]{1,0:T(8,128)(2,1)S(1)}, bf16[16,1024]{1,0:T(8,128)(2,1)S(1)}, u32[]{:S(2)}, u32[]{:S(2)}) collective-permute-start(bf16[16,1024]{1,0:T(8,128)(2,1)S(1)} %collective-permute-done.1), channel_id=1, source_target_pairs={{0,1},{1,2},{2,3},{3,0},{4,5},{5,6},{6,7},{7,4},{8,9},{9,10},{10,1... | collective-permute-start | bytes 98312 | tf_op jit(solution)/shard_map/ppermute | solution.py:100
  204.3 11.2 %all-to-all-start = ((f32[4,24,384]{2,1,0:T(8,128)}), f32[4,24,384]{2,1,0:T(8,128)S(1)}, u32[]{:S(2)}, u32[]{:S(2)}) async-start(f32[4,24,384]{2,1,0:T(8,128)} %all-reduce.6.cloned.1.call-done), calls=%async_computation.1 | async-start | bytes 294912 | tf_op jit(solution)/shard_map/all_to_all | solution.py:117
Sparse Core Ops, SparseCore 0:
  36.2 59.2 all-reduce.3
  101.4 32.6 reduce-scatter.1
  155.2 49.1 all-reduce.5
